TPU v7x, 256 devices: a whole 4x4x8 slice. The times are simulated.
256 devices in a mesh: shard: 16 (over z, core), tensor: 4 (over x), section: 4 (over y).
Axes of the slice: x: 4, y: 4, z: 8, core: 2. Of those that a mesh axis runs over, the one named last changes fastest.
Arguments:
- gradient: bfloat16 [6, 2048, 8192], P(None, ('tensor', 'section'), 'shard'), may hold values from -6 to 6
- basis: bfloat16 [6, 2048, 256], P(None, ('tensor', 'section')), may hold values from -6 to 6
- moment_m: float32 [6, 8192, 256], P(None, ('shard', 'tensor', 'section')), may hold values from -4 to 4
- moment_v: float32 [6, 8192, 256], P(None, ('shard', 'tensor', 'section')), may hold values from 0.002 to 0.02
Outputs:
- delta: bfloat16 [6, 2048, 8192], P(None, ('tensor', 'section'), 'shard')
- basis_new: bfloat16 [6, 2048, 256], P(None, ('tensor', 'section'))
- moment_m_new: float32 [6, 8192, 256], P(None, ('shard', 'tensor', 'section'))
- moment_v_new: float32 [6, 8192, 256], P(None, ('shard', 'tensor', 'section'))
All inputs are finite; a program needn't handle non-finite values. Where the computation divides by a largest or mean magnitude, that divisor is 1e-20 or more.
Results may differ from a plain program's by a relative error of at most 0.0049.
Values may be sent and summed in bfloat16 or wider, within the bound.
A program may use at most 64 MiB of HBM per device.

v0:
```python
import math
import jax
import jax.numpy as jnp
from jax import lax
from jax.sharding import PartitionSpec as P

D = 2048
NS_ITERS = 4
beta_one = 0.9
beta_two = 0.999
bias_one = 1.0 - 0.9**10
bias_two = 1.0 - 0.999**10
eps_adam = 1e-08
galore_gain = 4.0


def gram_total(iterate):
    local_gram = jnp.einsum("kmr,kms->krs", iterate, iterate, precision=lax.Precision.HIGHEST)
    return lax.psum(local_gram, ("tensor", "section"))


def orthogonal(subspace):
    gram_mat = gram_total(subspace)
    row_bound = jnp.max(jnp.sum(jnp.abs(gram_mat), axis=2), axis=1)[:, None, None] + 1e-06
    iterate = subspace / jnp.sqrt(row_bound)
    gram_mat = gram_mat / row_bound
    identity = jnp.eye(gram_mat.shape[1], dtype=jnp.float32)
    for turn_index in range(NS_ITERS):
        factor = 1.5 * identity - 0.5 * gram_mat
        iterate = jnp.einsum("kmr,krs->kms", iterate, factor, precision=lax.Precision.HIGHEST)
        if turn_index + 1 < NS_ITERS:
            gram_mat = gram_total(iterate)
    return iterate


def per_device(gradient, basis, moment_m, moment_v):
    width_root = math.sqrt(D)
    partial_low = jnp.einsum("kmn,kmr->knr", gradient, basis, preferred_element_type=jnp.float32)
    low_rank = (
        lax.psum_scatter(partial_low, ("tensor", "section"), scatter_dimension=1, tiled=True)
        / width_root
    )
    moment_m_new = beta_one * moment_m + (1.0 - beta_one) * low_rank
    moment_v_new = beta_two * moment_v + (1.0 - beta_two) * low_rank * low_rank
    step_low = (moment_m_new / bias_one / (jnp.sqrt(moment_v_new / bias_two) + eps_adam)).astype(
        jnp.bfloat16
    )
    rough_low = low_rank.astype(jnp.bfloat16)
    step_block, rough_block = (
        lax.all_gather(step_low, ("tensor", "section"), axis=1, tiled=True),
        lax.all_gather(rough_low, ("tensor", "section"), axis=1, tiled=True),
    )
    delta = (
        -galore_gain
        / width_root
        * jnp.einsum("kmr,knr->kmn", basis, step_block, preferred_element_type=jnp.float32)
    ).astype(jnp.bfloat16)
    subspace = jnp.einsum("kmn,knr->kmr", gradient, rough_block, preferred_element_type=jnp.float32)
    whole_sum = lax.psum(subspace, "shard")
    basis_new = (width_root * orthogonal(whole_sum)).astype(jnp.bfloat16)
    return (delta, basis_new, moment_m_new, moment_v_new)


def solution(mesh):
    placed = (
        P(None, ("tensor", "section"), "shard"),
        P(None, ("tensor", "section"), None),
        P(None, ("shard", "tensor", "section"), None),
        P(None, ("shard", "tensor", "section"), None),
    )
    return jax.shard_map(
        per_device,
        mesh=mesh,
        in_specs=placed,
        out_specs=(
            P(None, ("tensor", "section"), "shard"),
            P(None, ("tensor", "section"), None),
            P(None, ("shard", "tensor", "section"), None),
            P(None, ("shard", "tensor", "section"), None),
        ),
        check_vma=False,
    )
```

profile of v0, /device:TPU:32, one launch (start us, length us, event | category | flops | bytes accessed | tf_op | source)
XLA Modules:
  0.0 738.4 jit_solution(1374766177256162602)
XLA Ops:
  7.2 0.0 copy-start
  7.2 0.0 reduce-scatter.2.cloned.1.call-start
  7.2 1.1 copy-done
  8.3 3.3 fusion.37
  11.6 0.0 copy-start.3
  11.6 0.0 copy-start.4
  11.6 0.0 reduce-scatter.2.cloned.1.call-update
  11.6 0.0 all-gather.5.cloned.1.call-start
  11.6 84.4 %reduce-scatter.2.cloned.1.call-done = f32[6,32,256]{2,1,0:T(8,128)} async-done(((f32[6,512,256]{2,1,0:T(8,128)}), f32[6,32,256]{2,1,0:T(8,128)}) %reduce-scatter.2.cloned.1.call-update) | async-done | bytes 196624 | tf_op jit(solution)/shard_map/reduce_scatter | solution.py:40
  96.0 0.0 copy-done.3
  96.0 0.0 copy-done.4
  96.0 1.8 divide_convert_fusion
  97.8 0.0 all-gather.5.cloned.1.call-update
  97.9 0.0 all-reduce.6.cloned.1.call-start
  97.9 49.2 %all-gather.5.cloned.1.call-done = bf16[6,512,256]{2,1,0:T(8,128)(2,1)} async-done(((bf16[6,32,256]{2,1,0:T(8,128)(2,1)}), bf16[6,512,256]{2,1,0:T(8,128)(2,1)}) %all-gather.5.cloned.1.call-update) | async-done | bytes 1572880 | tf_op jit(solution)/shard_map/all_gather | solution.py:51
  147.2 2.9 convolution_bitcast_fusion
  150.1 0.0 all-reduce.6.cloned.1.call-update
  150.1 0.0 all-reduce.8.cloned.1.call-start
  150.2 108.3 %all-reduce.6.cloned.1.call-done = f32[6,128,256]{1,2,0:T(8,128)} async-done(((f32[6,128,256]{1,2,0:T(8,128)}), f32[6,128,256]{1,2,0:T(8,128)}) %all-reduce.6.cloned.1.call-update) | async-done | bytes 786448 | tf_op jit(solution)/shard_map/psum | solution.py:59
  258.5 3.9 fusion.38
  262.4 0.0 copy-start.1
  262.4 0.0 all-reduce.8.cloned.1.call-update
  262.5 0.0 all-reduce.10.cloned.1.call-start
  262.5 102.3 %all-reduce.8.cloned.1.call-done = f32[6,256,256]{2,1,0:T(8,128)} async-done(((f32[6,256,256]{2,1,0:T(8,128)}), f32[6,256,256]{2,1,0:T(8,128)}) %all-reduce.8.cloned.1.call-update) | async-done | bytes 1572880 | tf_op jit(solution)/shard_map/psum | solution.py:19
  364.8 1.7 abs_reduce_fusion
  366.5 0.1 reduce_max.9
  366.6 0.0 copy-done.1
  366.6 3.2 fusion.9
  369.8 2.6 fusion.39
  372.4 0.0 all-reduce.10.cloned.1.call-update
  372.4 0.0 all-reduce.12.cloned.1.call-start
  372.5 98.7 %all-reduce.10.cloned.1.call-done = f32[6,256,256]{2,1,0:T(8,128)} async-done(((f32[6,256,256]{2,1,0:T(8,128)}), f32[6,256,256]{2,1,0:T(8,128)}) %all-reduce.10.cloned.1.call-update) | async-done | bytes 1572880 | tf_op jit(solution)/shard_map/psum | solution.py:19
  471.1 2.6 fusion.6
  473.7 2.6 fusion.40
  476.3 0.0 all-reduce.12.cloned.1.call-update
  476.4 0.0 all-gather.3.cloned.1.call-start
  476.4 0.7 all-gather.3.cloned.1.call-update
  477.1 0.2 all-reduce.14.cloned.1.call-start
  477.3 97.7 %all-reduce.12.cloned.1.call-done = f32[6,256,256]{2,1,0:T(8,128)} async-done(((f32[6,256,256]{2,1,0:T(8,128)}), f32[6,256,256]{2,1,0:T(8,128)}) %all-reduce.12.cloned.1.call-update) | async-done | bytes 1572880 | tf_op jit(solution)/shard_map/psum | solution.py:19
  575.1 2.6 fusion.3
  577.6 2.6 fusion.41
  580.3 0.0 copy-start.2
  580.3 0.0 all-reduce.14.cloned.1.call-update
  580.3 46.1 %all-gather.3.cloned.1.call-done = bf16[6,512,256]{2,1,0:T(8,128)(2,1)} async-done(((bf16[6,32,256]{2,1,0:T(8,128)(2,1)}), bf16[6,512,256]{2,1,0:T(8,128)(2,1)}) %all-gather.3.cloned.1.call-update) | async-done | bytes 1572880 | tf_op jit(solution)/shard_map/all_gather | solution.py:50
  626.4 0.0 copy-done.2
  626.4 2.0 fusion.13
  628.3 1.2 copy.15
  629.5 98.7 %all-reduce.14.cloned.1.call-done = f32[6,256,256]{2,1,0:T(8,128)} async-done(((f32[6,256,256]{2,1,0:T(8,128)}), f32[6,256,256]{2,1,0:T(8,128)}) %all-reduce.14.cloned.1.call-update) | async-done | bytes 1572880 | tf_op jit(solution)/shard_map/psum | solution.py:19
  728.2 3.3 fusion.17
  (2 shorter events, 0.0 us)
Async XLA Ops:
  7.2 1.1 copy-start
  7.2 88.8 %reduce-scatter.2.cloned.1.call-start = ((), (), s32[]{:S(2)}) async-start(), calls=%async_computation.1 | async-start | bytes 3342336 | tf_op jit(solution)/shard_map/reduce_scatter | solution.py:40
  11.6 84.4 %copy-start.3 = (f32[6,32,256]{2,1,0:T(8,128)S(1)}, f32[6,32,256]{2,1,0:T(8,128)}, u32[]{:S(2)}) copy-start(f32[6,32,256]{2,1,0:T(8,128)} %param.6) | copy-start | bytes 589828
  11.6 84.4 %copy-start.4 = (f32[6,32,256]{2,1,0:T(8,128)S(1)}, f32[6,32,256]{2,1,0:T(8,128)}, u32[]{:S(2)}) copy-start(f32[6,32,256]{2,1,0:T(8,128)} %param.7) | copy-start | bytes 589828
  11.6 135.6 %all-gather.5.cloned.1.call-start = ((), (), s32[]{:S(2)}) async-start(), calls=%async_computation.3 | async-start | bytes 1671168 | tf_op jit(solution)/shard_map/all_gather | solution.py:51
  97.9 160.6 %all-reduce.6.cloned.1.call-start = ((), (), s32[]{:S(2)}) async-start(), calls=%async_computation.4 | async-start | bytes 1572864 | tf_op jit(solution)/shard_map/psum | solution.py:59
  150.1 214.7 %all-reduce.8.cloned.1.call-start = ((), (), s32[]{:S(2)}) async-start(), calls=%async_computation.5 | async-start | bytes 3145728 | tf_op jit(solution)/shard_map/psum | solution.py:19
  262.4 104.2 %copy-start.1 = (f32[6,128,256]{1,2,0:T(8,128)S(1)}, f32[6,128,256]{1,2,0:T(8,128)}, u32[]{:S(2)}) copy-start(f32[6,128,256]{1,2,0:T(8,128)} %all-reduce.6.cloned.1.call-done) | copy-start | bytes 2359300
  262.5 208.7 %all-reduce.10.cloned.1.call-start = ((), (), s32[]{:S(2)}) async-start(), calls=%async_computation.6 | async-start | bytes 3145728 | tf_op jit(solution)/shard_map/psum | solution.py:19
  372.4 202.6 %all-reduce.12.cloned.1.call-start = ((), (), s32[]{:S(2)}) async-start(), calls=%async_computation.7 | async-start | bytes 3145728 | tf_op jit(solution)/shard_map/psum | solution.py:19
  476.4 150.0 %all-gather.3.cloned.1.call-start = ((), (), s32[]{:S(2)}) async-start(), calls=%async_computation.2 | async-start | bytes 1671168 | tf_op jit(solution)/shard_map/all_gather | solution.py:50
  477.1 251.1 %all-reduce.14.cloned.1.call-start = ((), (), s32[]{:S(2)}) async-start(), calls=%async_computation.8 | async-start | bytes 3145728 | tf_op jit(solution)/shard_map/psum | solution.py:19
  580.3 46.1 %copy-start.2 = (bf16[6,128,256]{2,1,0:T(8,128)(2,1)S(1)}, bf16[6,128,256]{2,1,0:T(8,128)(2,1)}, u32[]{:S(2)}) copy-start(bf16[6,128,256]{2,1,0:T(8,128)(2,1)} %param.5) | copy-start | bytes 1179652
Sparse Core Ops, SparseCore 0:
  11.7 84.2 reduce-scatter.1
  99.1 48.0 all-gather.4
  150.2 108.2 all-reduce.5
  262.6 102.1 all-reduce.7
  372.6 98.5 all-reduce.9
  476.5 98.5 all-reduce.11
  578.1 48.1 all-gather.2
  629.7 98.5 all-reduce.13
where the time goes:
time: 739 us; the launch traced here: 738 us
  waiting for transfers between devices  686 us (93%)
  matrix products  31.6 us (4%)
  between operations  14.2 us (2%)
    psum x4, waiting for transfers between devices, gram_total(): return lax.psum(local_gram, ('tensor', 'section'))  397 us
    psum x1, waiting for transfers between devices, per_device(): whole_sum = lax.psum(subspace, 'shard')  108 us
    reduce_scatter x1, waiting for transfers between devices, per_device(): lax.psum_scatter(partial_low, ('tensor', 'section'), scatter_dimension=1,...  84.4 us
    all_gather x1, waiting for transfers between devices, per_device(): lax.all_gather(rough_low, ('tensor', 'section'), axis=1, tiled=True)  49.2 us
    all_gather x1, waiting for transfers between devices, per_device(): lax.all_gather(step_low, ('tensor', 'section'), axis=1, tiled=True)  46.1 us
  transfers between devices with their start and end apart: 8, of which 8 were waited for; matrix products, arithmetic and copies ran while one was open for 1% of the time, Pallas kernels for 0%

commit v1 on v0

--- a/solution.py
+++ b/solution.py
@@ -16,7 +16,7 @@
 
 def gram_total(iterate):
     local_gram = jnp.einsum("kmr,kms->krs", iterate, iterate, precision=lax.Precision.HIGHEST)
-    return lax.psum(local_gram, ("tensor", "section"))
+    return jnp.sum(lax.all_gather(local_gram, ("tensor", "section")), axis=0)
 
 
 def orthogonal(subspace):

time: 739 us -> 1000 us (1.35)
  waiting for transfers between devices: 686 us -> 918 us
  other arithmetic: 3.66 us -> 39.5 us
    all_gather x0 -> x4, waiting for transfers between devices: none -> 637 us  [gram_total(): return jnp.sum(lax.all_gather(local_gram, ('tensor', 'section')), axis=0)]
    psum x4 -> x0, waiting for transfers between devices: 397 us -> none  [gram_total(): return lax.psum(local_gram, ('tensor', 'section'))]
    reduce_sum x0 -> x4, other arithmetic: none -> 37.3 us  [gram_total(): return jnp.sum(lax.all_gather(local_gram, ('tensor', 'section')), axis=0)]
  transfers between devices with their start and end apart: 8 -> 8, of which waited for: 8 -> 8; matrix products, arithmetic and copies ran while one was open for 1% -> 2% of each run, Pallas kernels for 0% -> 0%
where the time goes in v1:
time: 1000 us
  waiting for transfers between devices  918 us (92%)
  other arithmetic  39.5 us (4%)
  matrix products  26 us (3%)
  between operations  14.2 us (1%)
    all_gather x4, waiting for transfers between devices, gram_total(): return jnp.sum(lax.all_gather(local_gram, ('tensor', 'section')), axis=0)  637 us
    psum x1, waiting for transfers between devices, per_device(): whole_sum = lax.psum(subspace, 'shard')  108 us
    reduce_scatter x1, waiting for transfers between devices, per_device(): lax.psum_scatter(partial_low, ('tensor', 'section'), scatter_dimension=1,...  84.3 us
    all_gather x1, waiting for transfers between devices, per_device(): lax.all_gather(rough_low, ('tensor', 'section'), axis=1, tiled=True)  49.3 us
    all_gather x1, waiting for transfers between devices, per_device(): lax.all_gather(step_low, ('tensor', 'section'), axis=1, tiled=True)  38.4 us
    reduce_sum x4, other arithmetic, gram_total(): return jnp.sum(lax.all_gather(local_gram, ('tensor', 'section')), axis=0)  37.3 us
  transfers between devices with their start and end apart: 8, of which 8 were waited for; matrix products, arithmetic and copies ran while one was open for 2% of the time, Pallas kernels for 0%

profile of v1, /device:TPU:32, one launch (start us, length us, event | category | flops | bytes accessed | tf_op | source)
XLA Modules:
  0.0 1001.5 jit_solution(12645789667474293930)
XLA Ops:
  7.2 0.0 copy-start
  7.2 0.0 reduce-scatter.2.cloned.1.call-start
  7.2 1.1 copy-done
  8.3 3.3 fusion.37
  11.6 0.0 copy-start.4
  11.6 0.0 copy-start.5
  11.6 0.0 reduce-scatter.2.cloned.1.call-update
  11.6 0.0 all-gather.13.cloned.1.call-start
  11.6 84.3 %reduce-scatter.2.cloned.1.call-done = f32[6,32,256]{2,1,0:T(8,128)} async-done(((f32[6,512,256]{2,1,0:T(8,128)}), f32[6,32,256]{2,1,0:T(8,128)}) %reduce-scatter.2.cloned.1.call-update) | async-done | bytes 196624 | tf_op jit(solution)/shard_map/reduce_scatter | solution.py:40
  96.0 0.0 copy-done.4
  96.0 0.0 copy-done.5
  96.0 1.8 divide_convert_fusion
  97.8 0.0 all-gather.13.cloned.1.call-update
  97.8 0.0 all-reduce.2.cloned.1.call-start
  97.9 49.3 %all-gather.13.cloned.1.call-done = bf16[6,512,256]{2,1,0:T(8,128)(2,1)} async-done(((bf16[6,32,256]{2,1,0:T(8,128)(2,1)}), bf16[6,512,256]{2,1,0:T(8,128)(2,1)}) %all-gather.13.cloned.1.call-update) | async-done | bytes 1572880 | tf_op jit(solution)/shard_map/all_gather | solution.py:51
  147.2 2.9 convolution_bitcast_fusion
  150.1 0.0 all-reduce.2.cloned.1.call-update
  150.1 0.0 all-gather.15.cloned.1.call-start
  150.2 108.3 %all-reduce.2.cloned.1.call-done = f32[6,128,256]{1,2,0:T(8,128)} async-done(((f32[6,128,256]{1,2,0:T(8,128)}), f32[6,128,256]{1,2,0:T(8,128)}) %all-reduce.2.cloned.1.call-update) | async-done | bytes 786448 | tf_op jit(solution)/shard_map/psum | solution.py:59
  258.5 4.0 fusion.38
  262.5 0.0 all-gather.15.cloned.1.call-update
  262.5 0.0 all-gather.17.cloned.1.call-start
  262.6 162.2 %all-gather.15.cloned.1.call-done = f32[96,256,256]{2,1,0:T(8,128)} async-done(((f32[6,256,256]{2,1,0:T(8,128)}), f32[96,256,256]{2,1,0:T(8,128)}) %all-gather.15.cloned.1.call-update) | async-done | bytes 25165840 | tf_op jit(solution)/shard_map/all_gather | solution.py:19
  424.8 9.3 reduce_sum.45
  434.1 0.0 copy-start.2
  434.2 0.3 abs_reduce_fusion
  434.4 0.1 reduce_max.9
  434.6 0.7 copy-done.2
  435.3 1.7 fusion.9
  437.0 2.7 fusion.39
  439.7 0.0 all-gather.17.cloned.1.call-update
  439.7 0.0 all-gather.19.cloned.1.call-start
  439.8 158.9 %all-gather.17.cloned.1.call-done = f32[96,256,256]{2,1,0:T(8,128)} async-done(((f32[6,256,256]{2,1,0:T(8,128)}), f32[96,256,256]{2,1,0:T(8,128)}) %all-gather.17.cloned.1.call-update) | async-done | bytes 25165840 | tf_op jit(solution)/shard_map/all_gather | solution.py:19
  598.7 9.3 reduce_sum.47
  608.0 1.2 fusion.6
  609.2 2.6 fusion.40
  611.8 0.0 all-gather.19.cloned.1.call-update
  611.8 0.0 all-gather.11.cloned.1.call-start
  611.9 0.7 all-gather.11.cloned.1.call-update
  612.6 0.2 all-gather.21.cloned.1.call-start
  612.8 158.0 %all-gather.19.cloned.1.call-done = f32[96,256,256]{2,1,0:T(8,128)} async-done(((f32[6,256,256]{2,1,0:T(8,128)}), f32[96,256,256]{2,1,0:T(8,128)}) %all-gather.19.cloned.1.call-update) | async-done | bytes 25165840 | tf_op jit(solution)/shard_map/all_gather | solution.py:19
  770.8 9.3 reduce_sum.48
  780.2 1.2 fusion.3
  781.3 2.6 fusion.41
  783.9 0.0 copy-start.3
  783.9 0.0 all-gather.21.cloned.1.call-update
  784.0 38.4 %all-gather.11.cloned.1.call-done = bf16[6,512,256]{2,1,0:T(8,128)(2,1)} async-done(((bf16[6,32,256]{2,1,0:T(8,128)(2,1)}), bf16[6,512,256]{2,1,0:T(8,128)(2,1)}) %all-gather.11.cloned.1.call-update) | async-done | bytes 1572880 | tf_op jit(solution)/shard_map/all_gather | solution.py:50
  822.4 0.0 copy-done.3
  822.4 2.0 fusion.13
  824.4 1.2 copy.28
  825.5 157.9 %all-gather.21.cloned.1.call-done = f32[96,256,256]{2,1,0:T(8,128)} async-done(((f32[6,256,256]{2,1,0:T(8,128)}), f32[96,256,256]{2,1,0:T(8,128)}) %all-gather.21.cloned.1.call-update) | async-done | bytes 25165840 | tf_op jit(solution)/shard_map/all_gather | solution.py:19
  983.4 0.0 copy-start.1
  983.4 9.3 reduce_sum.49
  992.8 1.9 fusion.17
  994.7 0.0 copy-done.1
  (2 shorter events, 0.0 us)
Async XLA Ops:
  7.2 1.1 copy-start
  7.2 88.8 %reduce-scatter.2.cloned.1.call-start = ((), (), s32[]{:S(2)}) async-start(), calls=%async_computation.1 | async-start | bytes 3342336 | tf_op jit(solution)/shard_map/reduce_scatter | solution.py:40
  11.6 84.4 %copy-start.4 = (f32[6,32,256]{2,1,0:T(8,128)S(1)}, f32[6,32,256]{2,1,0:T(8,128)}, u32[]{:S(2)}) copy-start(f32[6,32,256]{2,1,0:T(8,128)} %param.6) | copy-start | bytes 589828
  11.6 84.4 %copy-start.5 = (f32[6,32,256]{2,1,0:T(8,128)S(1)}, f32[6,32,256]{2,1,0:T(8,128)}, u32[]{:S(2)}) copy-start(f32[6,32,256]{2,1,0:T(8,128)} %param.7) | copy-start | bytes 589828
  11.6 135.6 %all-gather.13.cloned.1.call-start = ((), (), s32[]{:S(2)}) async-start(), calls=%async_computation.3 | async-start | bytes 1671168 | tf_op jit(solution)/shard_map/all_gather | solution.py:51
  97.8 160.7 %all-reduce.2.cloned.1.call-start = ((), (), s32[]{:S(2)}) async-start(), calls=%async_computation.4 | async-start | bytes 1572864 | tf_op jit(solution)/shard_map/psum | solution.py:59
  150.1 274.7 %all-gather.15.cloned.1.call-start = ((), (), s32[]{:S(2)}) async-start(), calls=%async_computation.5 | async-start | bytes 26738688 | tf_op jit(solution)/shard_map/all_gather | solution.py:19
  262.5 336.2 %all-gather.17.cloned.1.call-start = ((), (), s32[]{:S(2)}) async-start(), calls=%async_computation.6 | async-start | bytes 26738688 | tf_op jit(solution)/shard_map/all_gather | solution.py:19
  434.1 1.1 copy-start.2
  439.7 331.1 %all-gather.19.cloned.1.call-start = ((), (), s32[]{:S(2)}) async-start(), calls=%async_computation.7 | async-start | bytes 26738688 | tf_op jit(solution)/shard_map/all_gather | solution.py:19
  611.8 210.5 %all-gather.11.cloned.1.call-start = ((), (), s32[]{:S(2)}) async-start(), calls=%async_computation.2 | async-start | bytes 1671168 | tf_op jit(solution)/shard_map/all_gather | solution.py:50
  612.6 370.8 %all-gather.21.cloned.1.call-start = ((), (), s32[]{:S(2)}) async-start(), calls=%async_computation.8 | async-start | bytes 26738688 | tf_op jit(solution)/shard_map/all_gather | solution.py:19
  783.9 38.5 %copy-start.3 = (bf16[6,128,256]{2,1,0:T(8,128)(2,1)S(1)}, bf16[6,128,256]{2,1,0:T(8,128)(2,1)}, u32[]{:S(2)}) copy-start(bf16[6,128,256]{2,1,0:T(8,128)(2,1)} %param.5) | copy-start | bytes 1179652
  983.4 11.3 %copy-start.1 = (bf16[6,128,512]{2,1,0:T(8,128)(2,1)S(1)}, bf16[6,128,512]{2,1,0:T(8,128)(2,1)}, u32[]{:S(2)}) copy-start(bf16[6,128,512]{2,1,0:T(8,128)(2,1)} %param.4) | copy-start | bytes 2359300
Sparse Core Ops, SparseCore 0:
  11.7 84.2 reduce-scatter.1
  99.0 48.0 all-gather.12
  150.2 108.2 all-reduce.1
  262.6 162.1 all-gather.14
  439.9 158.8 all-gather.16
  612.0 158.8 all-gather.18
  773.9 48.4 all-gather.10
  824.9 158.5 all-gather.20
